TPU v7x, 32 devices: a whole 2x2x4 slice. The times are simulated.
32 devices in a mesh: tile: 4 (over x, core), blk: 8 (over z, y).
Axes of the slice: x: 2, y: 2, z: 4, core: 2. Of those that a mesh axis runs over, the one named last changes fastest.
Arguments:
- tokens: bfloat16 [32768, 384], P(('tile', 'blk')), may hold values from -52 to 52
- ln_gain: float32 [384], replicated, may hold values from 0.1 to 1.9
- route: int32 [32768, 2], P(('tile', 'blk')), may hold values from 0 to 15, all different within a row; in each aligned block of 1024 rows (0 to 1023, 1024 to 2047, ...) at most 192 rows name the same one
- gates: float32 [32768, 2], P(('tile', 'blk')), may hold values from 0.1 to 1
- w_gate: bfloat16 [16, 384, 1024], P('tile', 'blk'), may hold values from -0.3125 to 0.3125
- w_up: bfloat16 [16, 384, 1024], P('tile', 'blk'), may hold values from -0.3125 to 0.3125
- w_down: bfloat16 [16, 1024, 384], P('tile', 'blk'), may hold values from -0.1875 to 0.1875
- d_mixed: bfloat16 [32768, 384], P(('tile', 'blk')), may hold values from -6 to 6
Outputs:
- mixed: bfloat16 [32768, 384], P(('tile', 'blk'))
- grad_gates: float32 [32768, 2], P(('tile', 'blk'))
- grad_tokens: bfloat16 [32768, 384], P(('tile', 'blk'))
- grad_w_gate: float32 [16, 384, 1024], P('tile', 'blk')
- grad_w_up: float32 [16, 384, 1024], P('tile', 'blk')
- grad_w_down: float32 [16, 1024, 384], P('tile', 'blk')
Inputs may be any that keep to these rules, and one draw needn't show every extreme that they name: `route`: each row names 2 different experts; within the rows of one device no expert is named more than 192 times, a bound that some block reaches.
All inputs are finite; a program needn't handle non-finite values.
Results may differ from a plain program's by a relative error of at most 0.014.
Values may be sent and summed in bfloat16 or wider, within the bound.
A program may use at most 192 MiB of HBM per device.

v0:
```python
import jax
import jax.numpy as jnp
from jax import lax
from jax.sharding import PartitionSpec as P


def layer_norm(values, ln_gain):
    centre = jnp.mean(values, axis=-1, keepdims=True)
    centred = values - centre
    spread = jnp.mean(centred * centred, axis=-1, keepdims=True)
    return values * lax.rsqrt(spread + 1e-05) * ln_gain


def expert_forward(inputs_rows, weight_gate, weight_up, weight_down):
    gate_pre = jnp.einsum(
        "erd,edh->erh", inputs_rows, weight_gate, preferred_element_type=jnp.float32
    )
    up_pre = jnp.einsum("erd,edh->erh", inputs_rows, weight_up, preferred_element_type=jnp.float32)
    sigma_gate = jax.nn.sigmoid(gate_pre)
    hidden_act = (gate_pre * sigma_gate * up_pre).astype(jnp.bfloat16)
    expert_rows = jnp.einsum(
        "erh,ehd->erd", hidden_act, weight_down, preferred_element_type=jnp.float32
    )
    return (expert_rows.astype(jnp.bfloat16), gate_pre, up_pre, hidden_act)


def expert_backward(
    inputs_rows, d_rows, gate_pre, up_pre, hidden_act, weight_gate, weight_up, weight_down
):
    d_act = jnp.einsum("erd,ehd->erh", d_rows, weight_down, preferred_element_type=jnp.float32)
    sigma_gate = jax.nn.sigmoid(gate_pre)
    d_gate = (d_act * up_pre * sigma_gate * (1.0 + gate_pre * (1.0 - sigma_gate))).astype(
        jnp.bfloat16
    )
    d_up = (d_act * gate_pre * sigma_gate).astype(jnp.bfloat16)
    d_in = jnp.einsum(
        "erh,edh->erd", d_gate, weight_gate, preferred_element_type=jnp.float32
    ) + jnp.einsum("erh,edh->erd", d_up, weight_up, preferred_element_type=jnp.float32)
    grad_gate = jnp.einsum("erd,erh->edh", inputs_rows, d_gate, preferred_element_type=jnp.float32)
    grad_up = jnp.einsum("erd,erh->edh", inputs_rows, d_up, preferred_element_type=jnp.float32)
    grad_down = jnp.einsum("erh,erd->ehd", hidden_act, d_rows, preferred_element_type=jnp.float32)
    return (d_in.astype(jnp.bfloat16), grad_gate, grad_up, grad_down)


def on_device(tokens, ln_gain, route, gates, w_gate, w_up, w_down, d_mixed):
    tok_rows, features = tokens.shape
    top_picks = route.shape[1]
    per_tile = w_gate.shape[0]
    tile_count = lax.axis_size("tile")
    experts_all = per_tile * tile_count
    capacity = max(2, 3 * tok_rows * top_picks // (2 * experts_all))
    tokens_wide = tokens.astype(jnp.float32)
    normed = layer_norm(tokens_wide, ln_gain).astype(jnp.bfloat16)
    flat_route = route.reshape(-1)
    onehot = (flat_route[:, None] == lax.iota(jnp.int32, experts_all)[None, :]).astype(jnp.int32)
    slot_rank = jnp.sum((jnp.cumsum(onehot, axis=0) - 1) * onehot, axis=1)
    slot_index = flat_route * capacity + slot_rank

    def pack_slots(values):
        blank = jnp.zeros((experts_all * capacity, features), jnp.bfloat16)
        return blank.at[slot_index].set(values).reshape(tile_count, per_tile, capacity, features)

    def to_experts(packed):
        arrived = lax.all_to_all(packed, "tile", split_axis=0, concat_axis=2, tiled=True)[0]
        return arrived

    def from_experts(results):
        returned = lax.all_to_all(results[None], "tile", split_axis=2, concat_axis=0, tiled=True)
        picked = returned.reshape(experts_all * capacity, features)[slot_index]
        return picked.reshape(tok_rows, top_picks, features).astype(jnp.float32)

    weight_gate, weight_up, weight_down = (
        lax.all_gather(w_gate, "blk", axis=1, tiled=True),
        lax.all_gather(w_up, "blk", axis=1, tiled=True),
        lax.all_gather(w_down, "blk", axis=1, tiled=True),
    )
    inputs_rows = to_experts(pack_slots(jnp.repeat(normed, top_picks, axis=0)))
    expert_rows, gate_pre, up_pre, hidden_act = expert_forward(
        inputs_rows, weight_gate, weight_up, weight_down
    )
    expert_out = from_experts(expert_rows)
    mixed = jnp.sum(gates[:, :, None] * expert_out, axis=1).astype(jnp.bfloat16)
    d_wide = d_mixed.astype(jnp.float32)
    grad_gates = jnp.sum(d_wide[:, None, :] * expert_out, axis=-1)
    d_out = (
        (gates[:, :, None] * d_wide[:, None, :])
        .astype(jnp.bfloat16)
        .reshape(tok_rows * top_picks, features)
    )
    d_rows = to_experts(pack_slots(d_out))
    d_in, grad_gate, grad_up, grad_down = expert_backward(
        inputs_rows, d_rows, gate_pre, up_pre, hidden_act, weight_gate, weight_up, weight_down
    )
    d_normed = jnp.sum(from_experts(d_in), axis=1)

    def normalize(values):
        return layer_norm(values, ln_gain)

    unused, pullback = jax.vjp(normalize, tokens_wide)
    grad_tokens = pullback(d_normed)[0].astype(jnp.bfloat16)
    total_gate, total_up, total_down = (
        lax.psum_scatter(
            grad_gate.astype(jnp.bfloat16), "blk", scatter_dimension=1, tiled=True
        ).astype(jnp.float32),
        lax.psum_scatter(
            grad_up.astype(jnp.bfloat16), "blk", scatter_dimension=1, tiled=True
        ).astype(jnp.float32),
        lax.psum_scatter(
            grad_down.astype(jnp.bfloat16), "blk", scatter_dimension=1, tiled=True
        ).astype(jnp.float32),
    )
    return (mixed, grad_gates, grad_tokens, total_gate, total_up, total_down)


def solution(mesh):
    placed = (
        P(("tile", "blk"), None),
        P(),
        P(("tile", "blk"), None),
        P(("tile", "blk"), None),
        P("tile", "blk", None),
        P("tile", "blk", None),
        P("tile", "blk", None),
        P(("tile", "blk"), None),
    )
    return jax.shard_map(
        on_device,
        mesh=mesh,
        in_specs=placed,
        out_specs=(
            P(("tile", "blk"), None),
            P(("tile", "blk"), None),
            P(("tile", "blk"), None),
            P("tile", "blk", None),
            P("tile", "blk", None),
            P("tile", "blk", None),
        ),
        check_vma=False,
    )
```

profile of v0, /device:TPU:0, one launch (start us, length us, event | category | flops | bytes accessed | tf_op | source)
XLA Modules:
  0.0 456.1 jit_solution(16825820951956494859)
XLA Ops:
  10.6 4.6 reduce-window.6
  18.5 1.5 reshape.153
  20.1 11.6 %scatter_custom_fusion = bf16[3072,384]{1,0:T(8,128)(2,1)} fusion(s32[2048]{0:T(1024)S(1)} %bitcast.70, bf16[2048,384]{1,0:T(8,128)(2,1)} %reshape.153, bf16[]{:T(256)} %constant.10.clone.1), kind=kCustom, calls=%fused_computation.35 | custom fusion | bytes 2359808 | tf_op jit(solution)/shard_map/scatter | solution.py:61
  31.7 4.5 all-to-all-start
  36.2 1.0 copy.32
  37.3 1.3 mul.148
  38.6 3.6 mul.146
  42.2 5.4 %mul.150 = f32[2048,384]{1,0:T(8,128)} reshape(f32[1024,2,384]{2,1,0:T(2,128)} %mul.146) | data formatting | bytes 6291456 | tf_op jit(solution)/shard_map/mul | solution.py:84
  47.6 12.6 %scatter_custom_fusion.1 = bf16[3072,384]{1,0:T(8,128)(2,1)} fusion(s32[2048]{0:T(1024)S(1)} %bitcast.71, f32[2048,384]{1,0:T(8,128)} %mul.150, f32[2048]{0:T(1024)S(1)} %mul.148, bf16[]{:T(256)} %constant.10.clone.1), kind=kCustom, calls=%fused_computation.32 | custom fusion | flops 1572864 | bytes 5513218 | tf_op jit(solution)/shard_map/scatter | solution.py:61
  60.2 4.6 %all-to-all-done = bf16[4,4,192,384]{3,2,1,0:T(8,128)(2,1)S(1)} async-done(((bf16[4,4,192,384]{3,2,1,0:T(8,128)(2,1)}), bf16[4,4,192,384]{3,2,1,0:T(8,128)(2,1)S(1)}, u32[]{:S(2)}, u32[]{:S(2)}) %all-to-all-start) | async-done | bytes 2359328 | tf_op jit(solution)/shard_map/all_to_all | solution.py:64
  64.8 1.4 copy-done.1
  66.2 4.5 all-to-all-start.2
  70.9 1.9 copy.36
  72.9 26.3 %all-to-all-done.2 = bf16[4,4,192,384]{3,2,1,0:T(8,128)(2,1)} async-done(((bf16[4,4,192,384]{3,2,1,0:T(8,128)(2,1)}), bf16[4,4,192,384]{3,2,1,0:T(8,128)(2,1)}, u32[]{:S(2)}, u32[]{:S(2)}) %all-to-all-start.2) | async-done | bytes 2359328 | tf_op jit(solution)/shard_map/all_to_all | solution.py:64
  99.2 3.4 copy.40
  102.6 8.7 %fusion.21 = f32[4,768,1024]{2,1,0:T(8,128)} fusion(bf16[4,768,384]{2,1,0:T(8,128)(2,1)S(1)} %bitcast.58, bf16[4,384,1024]{2,1,0:T(8,128)(2,1)} %all-gather.4.cloned.1.call-done), kind=kOutput, calls=%fused_computation.53 | convolution fusion | flops 2415919104 | bytes 18087936 | tf_op jit(solution)/shard_map/erd,edh->erh/dot_general | solution.py:15
  111.3 22.6 %all-gather.6.cloned.1.call-done = bf16[4,384,1024]{2,1,0:T(8,128)(2,1)} async-done(((bf16[4,48,1024]{2,1,0:T(8,128)(2,1)}), bf16[4,384,1024]{2,1,0:T(8,128)(2,1)}) %all-gather.6.cloned.1.call-update) | async-done | bytes 3145744 | tf_op jit(solution)/shard_map/all_gather | solution.py:74
  133.9 8.3 %fusion.22 = f32[4,768,1024]{2,1,0:T(8,128)} fusion(bf16[4,768,384]{2,1,0:T(8,128)(2,1)S(1)} %bitcast.59, bf16[4,384,1024]{2,1,0:T(8,128)(2,1)} %all-gather.6.cloned.1.call-done), kind=kOutput, calls=%fused_computation.54 | convolution fusion | flops 2415919104 | bytes 18087936 | tf_op jit(solution)/shard_map/erd,edh->erh/dot_general | solution.py:18
  142.2 52.6 %all-gather.8.cloned.1.call-done = bf16[4,1024,384]{2,1,0:T(8,128)(2,1)} async-done(((bf16[4,128,384]{2,1,0:T(8,128)(2,1)}), bf16[4,1024,384]{2,1,0:T(8,128)(2,1)}) %all-gather.8.cloned.1.call-update) | async-done | bytes 3145744 | tf_op jit(solution)/shard_map/all_gather | solution.py:75
  194.8 18.0 %multiply_convert_fusion = (bf16[4,768,1024]{2,1,0:T(8,128)(2,1)}, bf16[4,768,1024]{2,1,0:T(8,128)(2,1)}, bf16[4,768,1024]{2,1,0:T(8,128)(2,1)}) fusion(f32[4,768,1024]{2,1,0:T(8,128)} %fusion.21, f32[4,768,1024]{2,1,0:T(8,128)} %fusion.22, bf16[4,768,384]{2,1,0:T(8,128)(2,1)} %bitcast.66, bf16[4,1024,384]{2,1,0:T(8,128)(2,1)} %all-gather.8.cloned.1.call-done), kind=kOutput, calls=%fused_computation.4 | convolution fusion | flops 2466250752 | bytes 49545216 | tf_op jit(solution)/shard_map/erd,ehd->erh/dot_general | solution.py:30
  212.8 7.1 %convolution_convert_fusion.2 = bf16[4,384,1024]{2,1,0:T(8,128)(2,1)} fusion(bf16[4,768,384]{2,1,0:T(8,128)(2,1)S(1)} %bitcast.60, bf16[4,768,1024]{2,1,0:T(8,128)(2,1)} %get-tuple-element.15), kind=kOutput, calls=%fused_computation.20 | convolution fusion | flops 2417491968 | bytes 11796480 | tf_op jit(solution)/shard_map/erd,erh->edh/dot_general | solution.py:39
  220.5 7.1 %convolution_convert_fusion.1 = bf16[4,384,1024]{2,1,0:T(8,128)(2,1)} fusion(bf16[4,768,384]{2,1,0:T(8,128)(2,1)S(1)} %bitcast.61, bf16[4,768,1024]{2,1,0:T(8,128)(2,1)} %get-tuple-element.14), kind=kOutput, calls=%fused_computation.19 | convolution fusion | flops 2417491968 | bytes 11796480 | tf_op jit(solution)/shard_map/erd,erh->edh/dot_general | solution.py:40
  227.7 1.6 copy-done.7
  229.3 8.0 %convolution_convert_fusion = bf16[4,1024,384]{2,1,0:T(8,128)(2,1)} fusion(bf16[4,768,1024]{2,1,0:T(8,128)(2,1)} %get-tuple-element.16, bf16[4,768,384]{2,1,0:T(8,128)(2,1)S(1)} %bitcast.67), kind=kOutput, calls=%fused_computation.18 | convolution fusion | flops 2417491968 | bytes 11796480 | tf_op jit(solution)/shard_map/erh,erd->ehd/dot_general | solution.py:41
  237.3 6.7 %fusion.23 = f32[4,768,384]{2,1,0:T(8,128)S(1)} fusion(bf16[4,768,1024]{2,1,0:T(8,128)(2,1)} %get-tuple-element.15, bf16[4,384,1024]{2,1,0:T(8,128)(2,1)} %all-gather.4.cloned.1.call-done), kind=kOutput, calls=%fused_computation.55 | convolution fusion | flops 2415919104 | bytes 14155776 | tf_op jit(solution)/shard_map/erh,edh->erd/dot_general | solution.py:36
  244.1 3.7 fusion
  247.8 3.2 copy.41
  251.0 3.6 all-to-all-start.3
  254.7 7.2 %convert_bitcast_fusion = bf16[1,4,768,384]{3,2,1,0:T(8,128)(2,1)S(1)} fusion(bf16[4,768,1024]{2,1,0:T(8,128)(2,1)} %get-tuple-element.16, bf16[4,1024,384]{2,1,0:T(8,128)(2,1)} %all-gather.8.cloned.1.call-done), kind=kOutput, calls=%fused_computation.17 | convolution fusion | flops 2417098752 | bytes 11796480 | tf_op jit(solution)/shard_map/erh,ehd->erd/dot_general | solution.py:21
  261.9 3.3 copy.37
  265.1 18.0 %all-to-all-done.3 = bf16[1,4,768,384]{3,1,0,2:T(4,128)(2,1)S(1)} async-done(((bf16[1,4,768,384]{3,1,0,2:T(4,128)(2,1)}), bf16[1,4,768,384]{3,1,0,2:T(4,128)(2,1)S(1)}, u32[]{:S(2)}, u32[]{:S(2)}) %all-to-all-start.3) | async-done | bytes 2359328 | tf_op jit(solution)/shard_map/all_to_all | solution.py:68
  283.1 1.4 copy-done.2
  284.5 4.7 %all-to-all-start.1 = ((bf16[1,4,768,384]{3,1,0,2:T(4,128)(2,1)}), bf16[1,4,768,384]{3,1,0,2:T(4,128)(2,1)}, u32[]{:S(2)}, u32[]{:S(2)}) async-start(bf16[1,4,768,384]{3,1,0,2:T(4,128)(2,1)} %copy.37), calls=%async_computation.1 | async-start | bytes 4718592 | tf_op jit(solution)/shard_map/all_to_all | solution.py:68
  289.2 2.6 convert_element_type.81
  292.2 9.0 %gather_fusion.1 = bf16[2048,384]{1,0:T(8,128)(2,1)} fusion(bf16[3072,384]{1,0:T(8,128)(2,1)S(1)} %bitcast.57, s32[2048]{0:T(1024)S(1)} %broadcast_clamp_fusion), kind=kCustom, calls=%fused_computation.1 | custom fusion | bytes 3153920 | tf_op jit(solution)/shard_map/gather | solution.py:69
  301.2 4.9 %reshape.132 = f32[1024,2,384]{2,1,0:T(2,128)} reshape(bf16[2048,384]{1,0:T(8,128)(2,1)} %gather_fusion.1) | data formatting | bytes 4718592 | tf_op jit(solution)/shard_map/convert_element_type | solution.py:70
  306.1 11.6 %all-to-all-done.1 = bf16[1,4,768,384]{3,1,0,2:T(4,128)(2,1)} async-done(((bf16[1,4,768,384]{3,1,0,2:T(4,128)(2,1)}), bf16[1,4,768,384]{3,1,0,2:T(4,128)(2,1)}, u32[]{:S(2)}, u32[]{:S(2)}) %all-to-all-start.1) | async-done | bytes 2359328 | tf_op jit(solution)/shard_map/all_to_all | solution.py:68
  317.7 2.1 copy.38
  319.9 9.1 %gather_fusion = bf16[2048,384]{1,0:T(8,128)(2,1)} fusion(bf16[3072,384]{1,0:T(8,128)(2,1)S(1)} %bitcast.56, s32[2048]{0:T(1024)S(1)} %broadcast_clamp_fusion), kind=kCustom, calls=%fused_computation | custom fusion | bytes 3153920 | tf_op jit(solution)/shard_map/gather | solution.py:69
  328.9 5.0 %reshape.131 = f32[1024,2,384]{2,1,0:T(2,128)} reshape(bf16[2048,384]{1,0:T(8,128)(2,1)} %gather_fusion) | data formatting | bytes 4718592 | tf_op jit(solution)/shard_map/convert_element_type | solution.py:70
  334.0 10.1 %multiply_reduce_fusion = (f32[1024,2]{1,0:T(8,128)S(1)}, bf16[1024,384]{1,0:T(8,128)(2,1)}) fusion(f32[1024,2,384]{2,1,0:T(2,128)} %reshape.131, f32[1024,384]{1,0:T(8,128)S(1)} %copy-done.4, f32[1024,2]{1,0:T(8,128)S(1)} %copy-done.5), kind=kLoop, calls=%fused_computation.10 | loop fusion | flops 2750464 | bytes 5521408 | tf_op jit(solution)/shard_map/reduce_sum | solution.py:84
  344.9 5.7 %reduce_sum.96 = f32[1024,384]{1,0:T(8,128)S(1)} reduce(f32[1024,2,384]{2,1,0:T(2,128)} %reshape.132, f32[]{:T(128)} %constant.25.clone.1), dimensions={1}, to_apply=%region_9.10 | reduce | flops 393216 | bytes 4718596 | tf_op jit(solution)/shard_map/reduce_sum | solution.py:94
  351.3 1.7 fusion.8
  353.0 2.0 convert_element_type.90
  355.0 15.0 %reduce-scatter.6.cloned.1.call-done = bf16[4,48,1024]{2,1,0:T(8,128)(2,1)} async-done(((bf16[4,384,1024]{2,1,0:T(8,128)(2,1)}), bf16[4,48,1024]{2,1,0:T(8,128)(2,1)}) %reduce-scatter.6.cloned.1.call-update) | async-done | bytes 393232 | tf_op jit(solution)/shard_map/reduce_scatter | solution.py:105
  370.0 2.0 convert_element_type.92
  372.0 75.1 %reduce-scatter.8.cloned.1.call-done = bf16[4,128,384]{2,1,0:T(8,128)(2,1)} async-done(((bf16[4,1024,384]{2,1,0:T(8,128)(2,1)}), bf16[4,128,384]{2,1,0:T(8,128)(2,1)}) %reduce-scatter.8.cloned.1.call-update) | async-done | bytes 393232 | tf_op jit(solution)/shard_map/reduce_scatter | solution.py:108
  447.1 1.9 convert_element_type.94
  (63 shorter events, 9.7 us)
Async XLA Ops:
  7.2 8.7 %copy-start = (bf16[1024,384]{1,0:T(8,128)(2,1)S(1)}, bf16[1024,384]{1,0:T(8,128)(2,1)}, u32[]{:S(2)}) copy-start(bf16[1024,384]{1,0:T(8,128)(2,1)} %param.8) | copy-start | bytes 2359300
  7.2 9.4 %copy-start.9 = (f32[384]{0:T(512)S(1)}, f32[384]{0:T(512)}, u32[]{:S(2)}) copy-start(f32[384]{0:T(512)} %param.9) | copy-start | bytes 4612
  7.2 95.4 %all-gather.4.cloned.1.call-start = ((), (), s32[]{:S(2)}) async-start(), calls=%async_computation.7 | async-start | bytes 3538944 | tf_op jit(solution)/shard_map/all_gather | solution.py:73
  7.9 126.0 %all-gather.6.cloned.1.call-start = ((), (), s32[]{:S(2)}) async-start(), calls=%async_computation.8 | async-start | bytes 3538944 | tf_op jit(solution)/shard_map/all_gather | solution.py:74
  8.7 186.1 %all-gather.8.cloned.1.call-start = ((), (), s32[]{:S(2)}) async-start(), calls=%async_computation.9 | async-start | bytes 3538944 | tf_op jit(solution)/shard_map/all_gather | solution.py:75
  10.3 6.5 %copy-start.8 = (s32[1024,2]{0,1:T(2,128)S(1)}, s32[1024,2]{0,1:T(2,128)}, u32[]{:S(2)}) copy-start(s32[1024,2]{0,1:T(2,128)} %param.10) | copy-start | bytes 24580
  31.7 4.5 copy-start.10
  31.7 33.1 %all-to-all-start = ((bf16[4,4,192,384]{3,2,1,0:T(8,128)(2,1)}), bf16[4,4,192,384]{3,2,1,0:T(8,128)(2,1)S(1)}, u32[]{:S(2)}, u32[]{:S(2)}) async-start(bf16[4,4,192,384]{3,2,1,0:T(8,128)(2,1)} %bitcast.65), calls=%async_computation | async-start | bytes 4718592 | tf_op jit(solution)/shard_map/all_to_all | solution.py:64
  64.8 1.4 copy-start.1
  66.2 33.0 %all-to-all-start.2 = ((bf16[4,4,192,384]{3,2,1,0:T(8,128)(2,1)}), bf16[4,4,192,384]{3,2,1,0:T(8,128)(2,1)}, u32[]{:S(2)}, u32[]{:S(2)}) async-start(bf16[4,4,192,384]{3,2,1,0:T(8,128)(2,1)} %bitcast.64), calls=%async_computation.2 | async-start | bytes 4718592 | tf_op jit(solution)/shard_map/all_to_all | solution.py:64
  70.7 282.4 %reduce-scatter.4.cloned.1.call-start = ((), (), s32[]{:S(2)}) async-start(), calls=%async_computation.10 | async-start | bytes 3538944 | tf_op jit(solution)/shard_map/reduce_scatter | solution.py:102
  219.9 150.1 %reduce-scatter.6.cloned.1.call-start = ((), (), s32[]{:S(2)}) async-start(), calls=%async_computation.11 | async-start | bytes 3538944 | tf_op jit(solution)/shard_map/reduce_scatter | solution.py:105
  227.6 1.7 copy-start.7
  227.6 219.5 %reduce-scatter.8.cloned.1.call-start = ((), (), s32[]{:S(2)}) async-start(), calls=%async_computation.12 | async-start | bytes 3538944 | tf_op jit(solution)/shard_map/reduce_scatter | solution.py:108
  237.2 6.7 %slice-start = ((s8[6291456]{0:T(1024)(128)(4,1)}), s8[2097152]{0:T(1024)(128)(4,1)S(1)}, s32[]{:S(2)}) async-start(s8[6291456]{0:T(1024)(128)(4,1)} %bitcast.74), calls=%async_computation.13 | async-start | bytes 4194304
  237.2 6.7 %copy-start.6 = (bf16[4,384,1024]{2,1,0:T(8,128)(2,1)S(1)}, bf16[4,384,1024]{2,1,0:T(8,128)(2,1)}, u32[]{:S(2)}) copy-start(bf16[4,384,1024]{2,1,0:T(8,128)(2,1)} %all-gather.6.cloned.1.call-done) | copy-start | bytes 9437188
  237.2 6.8 %slice-start.1 = ((s8[6291456]{0:T(1024)(128)(4,1)}), s8[4194304]{0:T(1024)(128)(4,1)S(1)}, s32[]{:S(2)}) async-start(s8[6291456]{0:T(1024)(128)(4,1)} %bitcast.74), calls=%async_computation.14 | async-start | bytes 8388608
  251.0 32.1 %all-to-all-start.3 = ((bf16[1,4,768,384]{3,1,0,2:T(4,128)(2,1)}), bf16[1,4,768,384]{3,1,0,2:T(4,128)(2,1)S(1)}, u32[]{:S(2)}, u32[]{:S(2)}) async-start(bf16[1,4,768,384]{3,1,0,2:T(4,128)(2,1)} %copy.41), calls=%async_computation.3 | async-start | bytes 4718592 | tf_op jit(solution)/shard_map/all_to_all | solution.py:68
  283.1 1.4 copy-start.2
  284.5 33.2 %all-to-all-start.1 = ((bf16[1,4,768,384]{3,1,0,2:T(4,128)(2,1)}), bf16[1,4,768,384]{3,1,0,2:T(4,128)(2,1)}, u32[]{:S(2)}, u32[]{:S(2)}) async-start(bf16[1,4,768,384]{3,1,0,2:T(4,128)(2,1)} %copy.37), calls=%async_computation.1 | async-start | bytes 4718592 | tf_op jit(solution)/shard_map/all_to_all | solution.py:68
  289.2 2.6 copy-start.3
  328.9 5.0 %copy-start.4 = (f32[1024,384]{1,0:T(8,128)S(1)}, f32[1024,384]{1,0:T(8,128)}, u32[]{:S(2)}) copy-start(f32[1024,384]{1,0:T(8,128)} %convert_element_type.81) | copy-start | bytes 4718596
  328.9 5.0 %copy-start.5 = (f32[1024,2]{1,0:T(8,128)S(1)}, f32[1024,2]{1,0:T(8,128)}, u32[]{:S(2)}) copy-start(f32[1024,2]{1,0:T(8,128)} %copy.32) | copy-start | bytes 24580
Sparse Core Ops, SparseCore 0:
  10.2 62.7 all-gather.3
  75.2 58.6 all-gather.5
  136.1 58.6 all-gather.7
  220.1 72.9 reduce-scatter.3
  296.5 73.4 reduce-scatter.5
  373.4 73.5 reduce-scatter.7
where the time goes:
time: 463 us; the launch traced here: 456 us
  waiting for transfers between devices  228 us (49%)
  local copies, waits for them, and re-layouts  75.3 us (16%)
  matrix products  74.9 us (16%)
  other arithmetic  45.1 us (10%)
  starting transfers between devices  18.2 us (4%)
  between operations  14.6 us (3%)
    reduce_scatter x1, waiting for transfers between devices, on_device(): lax.psum_scatter(grad_down.astype(jnp.bfloat16), 'blk', scatter_dimension...  75.1 us
    all_gather x1, waiting for transfers between devices, on_device(): lax.all_gather(w_down, 'blk', axis=1, tiled=True)  52.6 us
    all_to_all x2, waiting for transfers between devices, to_experts(): lax.all_to_all(packed, 'tile', split_axis=0, concat_axis=2, tiled=True)[0]  30.9 us
    all_to_all x2, waiting for transfers between devices, from_experts(): lax.all_to_all(results[None], 'tile', split_axis=2, concat_axis=0, tiled=...  29.6 us
    all_gather x1, waiting for transfers between devices, on_device(): lax.all_gather(w_up, 'blk', axis=1, tiled=True)  22.6 us
    gather x2, local copies, waits for them, and re-layouts, from_experts(): picked = returned.reshape(experts_all * capacity, features)[slot_index]  18.1 us
    dot_general x1, matrix products, expert_backward(): jnp.einsum('erd,ehd->erh', d_rows, weight_down, preferred_element_type=jn...  18 us
    reduce_scatter x1, waiting for transfers between devices, on_device(): lax.psum_scatter(grad_up.astype(jnp.bfloat16), 'blk', scatter_dimension=1...  15 us
  transfers between devices with their start and end apart: 10, of which 8 were waited for; matrix products, arithmetic and copies ran while one was open for 36% of the time, Pallas kernels for 0%

commit v1 on v0

--- a/solution.py
+++ b/solution.py
@@ -1,7 +1,18 @@
+import functools
 import jax
 import jax.numpy as jnp
 from jax import lax
 from jax.sharding import PartitionSpec as P
+
+
+def advance_terms_on(arr_in, array_dim, row_dim):
+    mat_out = lax.axis_size("tile")
+    f_now = jnp.stack(jnp.split(arr_in, mat_out, array_dim), axis=0)
+    small = lax.all_to_all(f_now, "tile", split_axis=0, concat_axis=0)
+    return jnp.concatenate(small, row_dim)
+
+
+_search_face = functools.partial(advance_terms_on, array_dim=2, row_dim=0)
 
 
 def layer_norm(values, ln_gain):
@@ -65,7 +76,7 @@
         return arrived
 
     def from_experts(results):
-        returned = lax.all_to_all(results[None], "tile", split_axis=2, concat_axis=0, tiled=True)
+        returned = _search_face(results[None])
         picked = returned.reshape(experts_all * capacity, features)[slot_index]
         return picked.reshape(tok_rows, top_picks, features).astype(jnp.float32)
 

time: 463 us -> 463 us (level)
  local copies, waits for them, and re-layouts: 75.3 us -> 63.2 us
  waiting for transfers between devices: 228 us -> 237 us
    reduce_scatter x1, waiting for transfers between devices: 15 us -> 21.8 us  [on_device(): lax.psum_scatter(grad_up.astype(jnp.bfloat16), 'blk', scatter_dimension=1...]
    broadcast_in_dim x2 -> x0, local copies, waits for them, and re-layouts: 6.48 us -> none  [from_experts(): results[None]]
  transfers between devices with their start and end apart: 10 -> 10, of which waited for: 8 -> 8; matrix products, arithmetic and copies ran while one was open for 36% -> 34% of each run, Pallas kernels for 0% -> 0%
where the time goes in v1:
time: 463 us; the launch traced here: 456 us
  waiting for transfers between devices  237 us (51%)
  matrix products  75 us (16%)
  local copies, waits for them, and re-layouts  63.2 us (14%)
  other arithmetic  48.7 us (11%)
  starting transfers between devices  18.2 us (4%)
  between operations  14.6 us (3%)
    reduce_scatter x1, waiting for transfers between devices, on_device(): lax.psum_scatter(grad_down.astype(jnp.bfloat16), 'blk', scatter_dimension...  75.2 us
    all_gather x1, waiting for transfers between devices, on_device(): lax.all_gather(w_down, 'blk', axis=1, tiled=True)  52.6 us
    all_to_all x2, waiting for transfers between devices, advance_terms_on(): small = lax.all_to_all(f_now, 'tile', split_axis=0, concat_axis=0)  31.2 us
    all_to_all x2, waiting for transfers between devices, to_experts(): lax.all_to_all(packed, 'tile', split_axis=0, concat_axis=2, tiled=True)[0]  30.9 us
    all_gather x1, waiting for transfers between devices, on_device(): lax.all_gather(w_up, 'blk', axis=1, tiled=True)  22.6 us
    reduce_scatter x1, waiting for transfers between devices, on_device(): lax.psum_scatter(grad_up.astype(jnp.bfloat16), 'blk', scatter_dimension=1...  21.8 us
    gather x2, local copies, waits for them, and re-layouts, from_experts(): picked = returned.reshape(experts_all * capacity, features)[slot_index]  18.2 us
    dot_general x1, matrix products, expert_backward(): jnp.einsum('erd,ehd->erh', d_rows, weight_down, preferred_element_type=jn...  18 us
  transfers between devices with their start and end apart: 10, of which 8 were waited for; matrix products, arithmetic and copies ran while one was open for 34% of the time, Pallas kernels for 0%

profile of v1, /device:TPU:0, one launch (start us, length us, event | category | flops | bytes accessed | tf_op | source)
XLA Modules:
  0.0 456.1 jit_solution(5669090185772937729)
XLA Ops:
  9.4 0.9 copy.30
  10.6 4.6 reduce-window.6
  17.7 0.8 broadcast_in_dim.10
  18.5 1.5 reshape.143
  20.1 11.6 %scatter_custom_fusion = bf16[3072,384]{1,0:T(8,128)(2,1)} fusion(s32[2048]{0:T(1024)S(1)} %bitcast.78, bf16[2048,384]{1,0:T(8,128)(2,1)} %reshape.143, bf16[]{:T(256)} %constant.10.clone.1), kind=kCustom, calls=%fused_computation.37 | custom fusion | bytes 2359808 | tf_op jit(solution)/shard_map/scatter | solution.py:72
  31.7 4.5 all-to-all-start
  36.2 1.0 copy.28
  37.3 1.3 mul.148
  38.6 3.6 mul.146
  42.2 5.4 %mul.150 = f32[2048,384]{1,0:T(8,128)} reshape(f32[1024,2,384]{2,1,0:T(2,128)} %mul.146) | data formatting | bytes 6291456 | tf_op jit(solution)/shard_map/mul | solution.py:95
  47.6 12.6 %scatter_custom_fusion.1 = bf16[3072,384]{1,0:T(8,128)(2,1)} fusion(s32[2048]{0:T(1024)S(1)} %bitcast.79, f32[2048,384]{1,0:T(8,128)} %mul.150, f32[2048]{0:T(1024)S(1)} %mul.148, bf16[]{:T(256)} %constant.10.clone.1), kind=kCustom, calls=%fused_computation.34 | custom fusion | flops 1572864 | bytes 5513218 | tf_op jit(solution)/shard_map/scatter | solution.py:72
  60.2 4.6 %all-to-all-done = bf16[4,4,192,384]{3,2,1,0:T(8,128)(2,1)S(1)} async-done(((bf16[4,4,192,384]{3,2,1,0:T(8,128)(2,1)}), bf16[4,4,192,384]{3,2,1,0:T(8,128)(2,1)S(1)}, u32[]{:S(2)}, u32[]{:S(2)}) %all-to-all-start) | async-done | bytes 2359328 | tf_op jit(solution)/shard_map/all_to_all | solution.py:75
  64.8 1.4 copy-done.1
  66.2 4.5 all-to-all-start.2
  70.9 1.9 copy.32
  72.9 26.3 %all-to-all-done.2 = bf16[4,4,192,384]{3,2,1,0:T(8,128)(2,1)} async-done(((bf16[4,4,192,384]{3,2,1,0:T(8,128)(2,1)}), bf16[4,4,192,384]{3,2,1,0:T(8,128)(2,1)}, u32[]{:S(2)}, u32[]{:S(2)}) %all-to-all-start.2) | async-done | bytes 2359328 | tf_op jit(solution)/shard_map/all_to_all | solution.py:75
  99.2 3.4 copy.34
  102.6 8.7 %fusion.21 = f32[4,768,1024]{2,1,0:T(8,128)} fusion(bf16[4,768,384]{2,1,0:T(8,128)(2,1)S(1)} %bitcast.67, bf16[4,384,1024]{2,1,0:T(8,128)(2,1)} %all-gather.4.cloned.1.call-done), kind=kOutput, calls=%fused_computation.63 | convolution fusion | flops 2415919104 | bytes 18087936 | tf_op jit(solution)/shard_map/erd,edh->erh/dot_general | solution.py:26
  111.3 22.6 %all-gather.6.cloned.1.call-done = bf16[4,384,1024]{2,1,0:T(8,128)(2,1)} async-done(((bf16[4,48,1024]{2,1,0:T(8,128)(2,1)}), bf16[4,384,1024]{2,1,0:T(8,128)(2,1)}) %all-gather.6.cloned.1.call-update) | async-done | bytes 3145744 | tf_op jit(solution)/shard_map/all_gather | solution.py:85
  133.9 8.3 %fusion.22 = f32[4,768,1024]{2,1,0:T(8,128)} fusion(bf16[4,768,384]{2,1,0:T(8,128)(2,1)S(1)} %bitcast.68, bf16[4,384,1024]{2,1,0:T(8,128)(2,1)} %all-gather.6.cloned.1.call-done), kind=kOutput, calls=%fused_computation.64 | convolution fusion | flops 2415919104 | bytes 18087936 | tf_op jit(solution)/shard_map/erd,edh->erh/dot_general | solution.py:29
  142.2 52.6 %all-gather.8.cloned.1.call-done = bf16[4,1024,384]{2,1,0:T(8,128)(2,1)} async-done(((bf16[4,128,384]{2,1,0:T(8,128)(2,1)}), bf16[4,1024,384]{2,1,0:T(8,128)(2,1)}) %all-gather.8.cloned.1.call-update) | async-done | bytes 3145744 | tf_op jit(solution)/shard_map/all_gather | solution.py:86
  194.8 18.0 %multiply_convert_fusion = (bf16[4,768,1024]{2,1,0:T(8,128)(2,1)}, bf16[4,768,1024]{2,1,0:T(8,128)(2,1)}, bf16[4,768,1024]{2,1,0:T(8,128)(2,1)}) fusion(f32[4,768,1024]{2,1,0:T(8,128)} %fusion.21, f32[4,768,1024]{2,1,0:T(8,128)} %fusion.22, bf16[4,768,384]{2,1,0:T(8,128)(2,1)} %bitcast.74, bf16[4,1024,384]{2,1,0:T(8,128)(2,1)} %all-gather.8.cloned.1.call-done), kind=kOutput, calls=%fused_computation.4 | convolution fusion | flops 2466250752 | bytes 49545216 | tf_op jit(solution)/shard_map/erd,ehd->erh/dot_general | solution.py:41
  212.8 7.1 %convolution_convert_fusion.2 = bf16[4,384,1024]{2,1,0:T(8,128)(2,1)} fusion(bf16[4,768,384]{2,1,0:T(8,128)(2,1)S(1)} %bitcast.69, bf16[4,768,1024]{2,1,0:T(8,128)(2,1)} %get-tuple-element.15), kind=kOutput, calls=%fused_computation.22 | convolution fusion | flops 2417491968 | bytes 11796480 | tf_op jit(solution)/shard_map/erd,erh->edh/dot_general | solution.py:50
  220.4 7.1 %convolution_convert_fusion.1 = bf16[4,384,1024]{2,1,0:T(8,128)(2,1)} fusion(bf16[4,768,384]{2,1,0:T(8,128)(2,1)S(1)} %bitcast.70, bf16[4,768,1024]{2,1,0:T(8,128)(2,1)} %get-tuple-element.14), kind=kOutput, calls=%fused_computation.21 | convolution fusion | flops 2417491968 | bytes 11796480 | tf_op jit(solution)/shard_map/erd,erh->edh/dot_general | solution.py:51
  227.6 1.6 copy-done.4
  229.2 8.0 %convolution_convert_fusion = bf16[4,1024,384]{2,1,0:T(8,128)(2,1)} fusion(bf16[4,768,1024]{2,1,0:T(8,128)(2,1)} %get-tuple-element.16, bf16[4,768,384]{2,1,0:T(8,128)(2,1)S(1)} %bitcast.75), kind=kOutput, calls=%fused_computation.20 | convolution fusion | flops 2417491968 | bytes 11796480 | tf_op jit(solution)/shard_map/erh,erd->ehd/dot_general | solution.py:52
  237.2 6.7 %fusion.23 = f32[4,768,384]{2,1,0:T(8,128)S(1)} fusion(bf16[4,768,1024]{2,1,0:T(8,128)(2,1)} %get-tuple-element.15, bf16[4,384,1024]{2,1,0:T(8,128)(2,1)} %all-gather.4.cloned.1.call-done), kind=kOutput, calls=%fused_computation.65 | convolution fusion | flops 2415919104 | bytes 14155776 | tf_op jit(solution)/shard_map/erh,edh->erd/dot_general | solution.py:47
  244.0 3.7 fusion
  248.0 1.8 pad_maximum_fusion.1
  249.8 3.6 all-to-all-start.3
  253.4 7.3 %convert_bitcast_fusion = bf16[1,4,768,384]{3,2,1,0:T(8,128)(2,1)S(1)} fusion(bf16[4,768,1024]{2,1,0:T(8,128)(2,1)} %get-tuple-element.16, bf16[4,1024,384]{2,1,0:T(8,128)(2,1)} %all-gather.8.cloned.1.call-done), kind=kOutput, calls=%fused_computation.19 | convolution fusion | flops 2417098752 | bytes 11796480 | tf_op jit(solution)/shard_map/erh,ehd->erd/dot_general | solution.py:32
  261.0 1.8 pad_maximum_fusion
  262.8 19.1 %all-to-all-done.3 = bf16[4,1,4,192,384]{4,3,2,1,0:T(8,128)(2,1)S(1)} async-done(((bf16[4,1,4,192,384]{4,3,2,1,0:T(8,128)(2,1)}), bf16[4,1,4,192,384]{4,3,2,1,0:T(8,128)(2,1)S(1)}, u32[]{:S(2)}, u32[]{:S(2)}) %all-to-all-start.3) | async-done | bytes 2359328 | tf_op jit(solution)/shard_map/all_to_all | solution.py:11
  281.8 4.7 %all-to-all-start.1 = ((bf16[4,1,4,192,384]{4,3,2,1,0:T(8,128)(2,1)}), bf16[4,1,4,192,384]{4,3,2,1,0:T(8,128)(2,1)}, u32[]{:S(2)}, u32[]{:S(2)}) async-start(bf16[4,1,4,192,384]{4,3,2,1,0:T(8,128)(2,1)} %pad_maximum_fusion), calls=%async_computation.1 | async-start | bytes 4718592 | tf_op jit(solution)/shard_map/all_to_all | solution.py:11
  286.5 2.4 convert_element_type.81
  289.0 9.0 %gather_fusion.1 = bf16[2048,384]{1,0:T(8,128)(2,1)} fusion(bf16[3072,384]{1,0:T(8,128)(2,1)S(1)} %bitcast.66, s32[2048]{0:T(1024)S(1)} %broadcast_clamp_fusion), kind=kCustom, calls=%fused_computation.1 | custom fusion | bytes 3153920 | tf_op jit(solution)/shard_map/gather | solution.py:80
  298.0 4.9 %reshape.122 = f32[1024,2,384]{2,1,0:T(2,128)} reshape(bf16[2048,384]{1,0:T(8,128)(2,1)} %gather_fusion.1) | data formatting | bytes 4718592 | tf_op jit(solution)/shard_map/convert_element_type | solution.py:81
  302.9 12.2 %all-to-all-done.1 = bf16[4,1,4,192,384]{4,3,2,1,0:T(8,128)(2,1)} async-done(((bf16[4,1,4,192,384]{4,3,2,1,0:T(8,128)(2,1)}), bf16[4,1,4,192,384]{4,3,2,1,0:T(8,128)(2,1)}, u32[]{:S(2)}, u32[]{:S(2)}) %all-to-all-start.1) | async-done | bytes 2359328 | tf_op jit(solution)/shard_map/all_to_all | solution.py:11
  315.0 9.2 %gather_fusion = bf16[2048,384]{1,0:T(8,128)(2,1)S(1)} fusion(bf16[3072,384]{1,0:T(8,128)(2,1)} %bitcast.12, s32[2048]{0:T(1024)S(1)} %broadcast_clamp_fusion), kind=kCustom, calls=%fused_computation | custom fusion | bytes 3153920 | tf_op jit(solution)/shard_map/gather | solution.py:80
  324.3 2.7 reshape.121
  327.0 10.2 %multiply_reduce_fusion = (f32[1024,2]{1,0:T(8,128)S(1)}, bf16[1024,384]{1,0:T(8,128)(2,1)}) fusion(f32[1024,2,384]{2,1,0:T(2,128)} %reshape.121, f32[1024,384]{1,0:T(8,128)} %convert_element_type.81, f32[1024,2]{1,0:T(8,128)S(1)} %copy-done.2), kind=kLoop, calls=%fused_computation.10 | loop fusion | flops 2750464 | bytes 5521408 | tf_op jit(solution)/shard_map/reduce_sum | solution.py:95
  338.0 5.7 %reduce_sum.96 = f32[1024,384]{1,0:T(8,128)S(1)} reduce(f32[1024,2,384]{2,1,0:T(2,128)} %reshape.122, f32[]{:T(128)} %constant.25.clone.1), dimensions={1}, to_apply=%region_9.10 | reduce | flops 393216 | bytes 4718596 | tf_op jit(solution)/shard_map/reduce_sum | solution.py:105
  344.5 1.7 fusion.8
  346.2 2.0 convert_element_type.90
  348.1 21.8 %reduce-scatter.6.cloned.1.call-done = bf16[4,48,1024]{2,1,0:T(8,128)(2,1)} async-done(((bf16[4,384,1024]{2,1,0:T(8,128)(2,1)}), bf16[4,48,1024]{2,1,0:T(8,128)(2,1)}) %reduce-scatter.6.cloned.1.call-update) | async-done | bytes 393232 | tf_op jit(solution)/shard_map/reduce_scatter | solution.py:116
  370.0 2.0 convert_element_type.92
  371.9 75.2 %reduce-scatter.8.cloned.1.call-done = bf16[4,128,384]{2,1,0:T(8,128)(2,1)} async-done(((bf16[4,1024,384]{2,1,0:T(8,128)(2,1)}), bf16[4,128,384]{2,1,0:T(8,128)(2,1)}) %reduce-scatter.8.cloned.1.call-update) | async-done | bytes 393232 | tf_op jit(solution)/shard_map/reduce_scatter | solution.py:119
  447.1 1.9 convert_element_type.94
  (57 shorter events, 8.0 us)
Async XLA Ops:
  7.2 8.7 %copy-start = (bf16[1024,384]{1,0:T(8,128)(2,1)S(1)}, bf16[1024,384]{1,0:T(8,128)(2,1)}, u32[]{:S(2)}) copy-start(bf16[1024,384]{1,0:T(8,128)(2,1)} %param.8) | copy-start | bytes 2359300
  7.2 9.4 %copy-start.6 = (f32[384]{0:T(512)S(1)}, f32[384]{0:T(512)}, u32[]{:S(2)}) copy-start(f32[384]{0:T(512)} %param.9) | copy-start | bytes 4612
  7.2 95.4 %all-gather.4.cloned.1.call-start = ((), (), s32[]{:S(2)}) async-start(), calls=%async_computation.7 | async-start | bytes 3538944 | tf_op jit(solution)/shard_map/all_gather | solution.py:84
  7.9 126.0 %all-gather.6.cloned.1.call-start = ((), (), s32[]{:S(2)}) async-start(), calls=%async_computation.8 | async-start | bytes 3538944 | tf_op jit(solution)/shard_map/all_gather | solution.py:85
  8.7 186.1 %all-gather.8.cloned.1.call-start = ((), (), s32[]{:S(2)}) async-start(), calls=%async_computation.9 | async-start | bytes 3538944 | tf_op jit(solution)/shard_map/all_gather | solution.py:86
  10.3 6.5 %copy-start.5 = (s32[1024,2]{0,1:T(2,128)S(1)}, s32[1024,2]{0,1:T(2,128)}, u32[]{:S(2)}) copy-start(s32[1024,2]{0,1:T(2,128)} %param.10) | copy-start | bytes 24580
  31.7 4.5 copy-start.7
  31.7 33.1 %all-to-all-start = ((bf16[4,4,192,384]{3,2,1,0:T(8,128)(2,1)}), bf16[4,4,192,384]{3,2,1,0:T(8,128)(2,1)S(1)}, u32[]{:S(2)}, u32[]{:S(2)}) async-start(bf16[4,4,192,384]{3,2,1,0:T(8,128)(2,1)} %bitcast.73), calls=%async_computation | async-start | bytes 4718592 | tf_op jit(solution)/shard_map/all_to_all | solution.py:75
  64.8 1.4 copy-start.1
  66.2 33.0 %all-to-all-start.2 = ((bf16[4,4,192,384]{3,2,1,0:T(8,128)(2,1)}), bf16[4,4,192,384]{3,2,1,0:T(8,128)(2,1)}, u32[]{:S(2)}, u32[]{:S(2)}) async-start(bf16[4,4,192,384]{3,2,1,0:T(8,128)(2,1)} %bitcast.72), calls=%async_computation.2 | async-start | bytes 4718592 | tf_op jit(solution)/shard_map/all_to_all | solution.py:75
  70.7 275.5 %reduce-scatter.4.cloned.1.call-start = ((), (), s32[]{:S(2)}) async-start(), calls=%async_computation.10 | async-start | bytes 3538944 | tf_op jit(solution)/shard_map/reduce_scatter | solution.py:113
  219.9 150.0 %reduce-scatter.6.cloned.1.call-start = ((), (), s32[]{:S(2)}) async-start(), calls=%async_computation.11 | async-start | bytes 3538944 | tf_op jit(solution)/shard_map/reduce_scatter | solution.py:116
  227.5 1.7 copy-start.4
  227.6 219.6 %reduce-scatter.8.cloned.1.call-start = ((), (), s32[]{:S(2)}) async-start(), calls=%async_computation.12 | async-start | bytes 3538944 | tf_op jit(solution)/shard_map/reduce_scatter | solution.py:119
  237.2 6.8 %slice-start = ((s8[6291456]{0:T(1024)(128)(4,1)}), s8[2097152]{0:T(1024)(128)(4,1)S(1)}, s32[]{:S(2)}) async-start(s8[6291456]{0:T(1024)(128)(4,1)} %bitcast.82), calls=%async_computation.13 | async-start | bytes 4194304
  237.2 6.7 %copy-start.3 = (bf16[4,384,1024]{2,1,0:T(8,128)(2,1)S(1)}, bf16[4,384,1024]{2,1,0:T(8,128)(2,1)}, u32[]{:S(2)}) copy-start(bf16[4,384,1024]{2,1,0:T(8,128)(2,1)} %all-gather.6.cloned.1.call-done) | copy-start | bytes 9437188
  237.2 6.8 %slice-start.1 = ((s8[6291456]{0:T(1024)(128)(4,1)}), s8[4194304]{0:T(1024)(128)(4,1)S(1)}, s32[]{:S(2)}) async-start(s8[6291456]{0:T(1024)(128)(4,1)} %bitcast.82), calls=%async_computation.14 | async-start | bytes 8388608
  249.8 32.1 %all-to-all-start.3 = ((bf16[4,1,4,192,384]{4,3,2,1,0:T(8,128)(2,1)}), bf16[4,1,4,192,384]{4,3,2,1,0:T(8,128)(2,1)S(1)}, u32[]{:S(2)}, u32[]{:S(2)}) async-start(bf16[4,1,4,192,384]{4,3,2,1,0:T(8,128)(2,1)} %pad_maximum_fusion.1), calls=%async_computation.3 | async-start | bytes 4718592 | tf_op jit(solution)/shard_map/all_to_all | solution.py:11
  281.8 33.2 %all-to-all-start.1 = ((bf16[4,1,4,192,384]{4,3,2,1,0:T(8,128)(2,1)}), bf16[4,1,4,192,384]{4,3,2,1,0:T(8,128)(2,1)}, u32[]{:S(2)}, u32[]{:S(2)}) async-start(bf16[4,1,4,192,384]{4,3,2,1,0:T(8,128)(2,1)} %pad_maximum_fusion), calls=%async_computation.1 | async-start | bytes 4718592 | tf_op jit(solution)/shard_map/all_to_all | solution.py:11
  324.2 2.7 copy-start.2
Sparse Core Ops, SparseCore 0:
  10.2 62.7 all-gather.3
  75.2 58.6 all-gather.5
  136.1 58.6 all-gather.7
  220.1 72.9 reduce-scatter.3
  296.5 73.4 reduce-scatter.5
  373.4 73.6 reduce-scatter.7
